TPU v7x, 32 devices: a whole 2x2x4 slice. The times are simulated.
32 devices in a mesh: sec: 4 (over y, x), tile: 8 (over z, core).
Axes of the slice: x: 2, y: 2, z: 4, core: 2. Of those that a mesh axis runs over, the one named last changes fastest.
Arguments:
- displacement: float32 [2, 16, 256, 256], P(None, 'sec', 'tile'), may hold values from -3 to 3
- coupling: float32 [4, 16, 256, 256], P(None, 'sec', 'tile'), may hold values from 0.1 to 1
- matches: float32 [4, 2, 16, 256, 256], P(None, None, 'sec', 'tile'), may hold values from -3 to 3
- step_sizes: float32 [2, 8], replicated, may hold values from 0.1 to 0.35
- restarts: int32 [2, 8], replicated, may hold values 0 or 1
- images: float32 [4, 64, 256, 256], P('sec', 'tile'), may hold values from 0 to 1
- block_anchor: int32 [4, 64], P('sec', 'tile'), may hold values from 0 to 32767
- block_dest: int32 [4, 64, 1], P('sec', 'tile'), may hold values from 0 to 7; in each aligned block of 8 rows (0 to 7, 8 to 15, ..., all dimensions but the last counted through in order) at most 2 rows name the same one
- block_slot: int32 [4, 64], P('sec', 'tile'), may hold values from 0 to 1
- block_offset: int32 [4, 64, 2], P('sec', 'tile'), may hold values from 0 to 128
- block_count: int32 [4, 8], P('sec', 'tile'), may hold values from 6 to 8, as said below
Outputs:
- aligned: float32 [2, 16, 256, 256], P(None, 'sec', 'tile')
- spans: float32 [64, 384, 384], P(('sec', 'tile'))
Inputs may be any that keep to these rules, and one draw needn't show every extreme that they name: `block_dest`: no tile index is named by more than 2 of the block slots of one device, and 2 is reached. `block_count`: some device uses all 8 slots.
All inputs are finite; a program needn't handle non-finite values.
Results may differ from a plain program's by a relative error of at most 0.0003.
Values sent between devices are 32-bit elements; how exact they have to be, the bound alone decides.
A program may use at most 128 MiB of HBM per device.

v0:
```python
import jax
import jax.numpy as jnp
from jax import lax
from jax.sharding import PartitionSpec as P

OUTER = 2
FIRE_STEPS = 8
BPP = 256
CH = 384
SPAN_DEV = 2


STIFFNESS = 1.0
MIXING = 0.1
EPSILON = 1e-06
SPEED_CAP = 0.1
PRECISE = lax.Precision.HIGHEST


def with_halo(array, sides, width):
    for axis, dim in sides:
        size, length = (lax.axis_size(axis), array.shape[dim])
        up = [(i, (i + 1) % size) for i in range(size - 1)]
        down = [(j, i) for i, j in up]
        last = lax.slice_in_dim(array, length - width, length, axis=dim)
        leading = lax.slice_in_dim(array, 0, width, axis=dim)
        before = lax.ppermute(last, axis, up)
        after = lax.ppermute(leading, axis, down)
        array = jnp.concatenate([before, array, after], axis=dim)
    return array


def forces(current, refer, coupling, matches, first_sec, sections_all):
    strain = current - refer
    rimmed = with_halo(strain, (("tile", 2),), 1)
    sides = jnp.pad(strain, ((0, 0), (0, 0), (0, 0), (1, 1)))
    summed = STIFFNESS * (
        rimmed[:, :, 2:] + rimmed[:, :, :-2] + sides[..., 2:] + sides[..., :-2] - 4.0 * strain
    )
    stacked = with_halo(current, (("sec", 1),), 2)
    sections_dev = current.shape[1]
    section = first_sec + jnp.arange(sections_dev)
    for which_k, reach in enumerate((-2, -1, 1, 2)):
        beside = stacked[:, 2 + reach : 2 + reach + sections_dev]
        usable = ((section + reach >= 0) & (section + reach < sections_all)).astype(jnp.float32)
        summed = summed + usable[None, :, None, None] * coupling[which_k][None] * (
            beside + matches[which_k] - current
        )
    return summed


def hat_rows(shift, size, source):
    row_pos = jnp.arange(size).astype(jnp.float32)[None, :, None]
    src_pos = jnp.arange(source).astype(jnp.float32)[None, None, :]
    return jnp.maximum(0.0, 1.0 - jnp.abs(row_pos - src_pos - shift[:, None, None]))


def warp_blocks(blocks_in, shift_y, shift_x):
    row_hats = hat_rows(shift_y, CH, BPP)
    col_hats = hat_rows(shift_x, CH, BPP)
    halfway = jnp.einsum("bij,bkj->bik", blocks_in, col_hats, precision=PRECISE)
    return jnp.einsum("bri,bik->brk", row_hats, halfway, precision=PRECISE)


def body(
    displacement,
    coupling,
    matches,
    step_sizes,
    restarts,
    images,
    block_anchor,
    block_dest,
    block_slot,
    block_offset,
    block_count,
):
    sections_dev = displacement.shape[1]
    first_sec = lax.axis_index("sec") * sections_dev
    sections_all = sections_dev * lax.axis_size("sec")
    node_total = 2.0 * sections_all * displacement.shape[3] * displacement.shape[3]
    current = displacement
    refer = displacement
    velocity = jnp.zeros_like(displacement)
    for outer_step in range(OUTER):
        for inner_step in range(FIRE_STEPS):
            delta = step_sizes[outer_step, inner_step]
            push = forces(current, refer, coupling, matches, first_sec, sections_all)
            velocity = velocity + delta * push
            speed_sq, push_sq = lax.psum(
                (jnp.sum(velocity * velocity), jnp.sum(push * push)), ("sec", "tile")
            )
            ratio = jnp.sqrt(speed_sq + EPSILON) / jnp.sqrt(push_sq + EPSILON)
            limit = jnp.minimum(1.0, SPEED_CAP / jnp.sqrt(speed_sq / node_total + EPSILON))
            retain = 1.0 - restarts[outer_step, inner_step].astype(jnp.float32)
            velocity = limit * retain * ((1.0 - MIXING) * velocity + MIXING * ratio * push)
            current = current + delta * velocity
        refer = current
        velocity = jnp.zeros_like(current)
    flat_disp = current.reshape(2, -1)
    moved = jnp.take(flat_disp, block_anchor[0], axis=1)
    blocks_here = block_anchor.shape[1]
    usable = (jnp.arange(blocks_here) < block_count[0, 0]).astype(jnp.float32)
    offsets = block_offset[0].astype(jnp.float32)
    shift_y = offsets[:, 0] + moved[0]
    shift_x = offsets[:, 1] + moved[1]
    owners = block_dest[0, :, 0]
    slot_hot = (block_slot[0][:, None] == jnp.arange(SPAN_DEV)[None, :]).astype(
        jnp.float32
    ) * usable[:, None]
    tiles = lax.axis_size("tile")
    capacity = max(2, 2 * blocks_here // tiles)
    owner_hot = (owners[:, None] == jnp.arange(tiles)[None, :]).astype(jnp.int32)
    rank_all = jnp.cumsum(owner_hot, axis=0) - owner_hot
    rank_own = jnp.sum(rank_all * owner_hot, axis=1)
    position = owners * capacity + rank_own
    placer = (position[None, :] == jnp.arange(tiles * capacity)[:, None]).astype(jnp.float32)
    send_blocks = jnp.einsum("sb,bij->sij", placer, images[0], precision=PRECISE).reshape(
        tiles, capacity, BPP, BPP
    )
    shifts_both = jnp.stack([shift_y, shift_x], axis=1)
    send_shift = jnp.dot(placer, shifts_both, precision=PRECISE).reshape(tiles, capacity, 2)
    send_select = jnp.dot(placer, slot_hot, precision=PRECISE).reshape(tiles, capacity, SPAN_DEV)
    blocks_in = lax.all_to_all(send_blocks, "tile", split_axis=0, concat_axis=0, tiled=True)
    shift_in = lax.all_to_all(send_shift, "tile", split_axis=0, concat_axis=0, tiled=True)
    select_in = lax.all_to_all(send_select, "tile", split_axis=0, concat_axis=0, tiled=True)
    sources = blocks_in.shape[0]
    items = blocks_in.shape[1]
    drawn = warp_blocks(
        blocks_in.reshape(sources * items, BPP, BPP),
        shift_in[..., 0].reshape(-1),
        shift_in[..., 1].reshape(-1),
    )
    drawn = drawn.reshape(sources, items, CH, CH)
    pieces = jnp.einsum("skc,skrq->kcrq", select_in, drawn, precision=PRECISE)
    spans = jnp.sum(pieces, axis=0)
    return (current, spans)


def solution(mesh):
    placed = (
        P(None, "sec", "tile", None),
        P(None, "sec", "tile", None),
        P(None, None, "sec", "tile", None),
        P(),
        P(),
        P("sec", "tile", None, None),
        P("sec", "tile"),
        P("sec", "tile", None),
        P("sec", "tile"),
        P("sec", "tile", None),
        P("sec", "tile"),
    )
    return jax.shard_map(
        body,
        mesh=mesh,
        in_specs=placed,
        out_specs=(P(None, "sec", "tile", None), P(("sec", "tile"), None, None)),
        check_vma=False,
    )
```

profile of v0, /device:TPU:0, one launch (start us, length us, event | category | flops | bytes accessed | tf_op | source)
XLA Modules:
  0.0 1110.0 jit_solution(523799049433969451)
XLA Ops:
  1.8 4.9 collective-permute-start.2
  9.2 2.0 fusion.457
  11.8 2.0 fusion.458
  16.2 3.0 collective-permute-start.1
  20.0 3.0 multiply_reduce_fusion.30
  23.0 43.6 %all-reduce.31 = (f32[]{:T(128)}, f32[]{:T(128)}) all-reduce(f32[]{:T(128)} %get-tuple-element.41, f32[]{:T(128)} %get-tuple-element.40), channel_id=1, replica_groups=mesh['sec'=4,'tile'=8] {'sec','tile'}, use_global_device_ids=true, to_apply=%region_1.2 | all-reduce | flops 2 | bytes 16 | tf_op jit(solution)/shard_map/psum | solution.py:90
  69.4 4.2 collective-permute-start.6
  76.2 3.0 collective-permute-start.5
  81.0 2.4 multiply_reduce_fusion.28
  83.4 42.6 %all-reduce.30 = (f32[]{:T(128)}, f32[]{:T(128)}) all-reduce(f32[]{:T(128)} %get-tuple-element.39, f32[]{:T(128)} %get-tuple-element.38), channel_id=1, replica_groups=mesh['sec'=4,'tile'=8] {'sec','tile'}, use_global_device_ids=true, to_apply=%region_5.6 | all-reduce | flops 2 | bytes 16 | tf_op jit(solution)/shard_map/psum | solution.py:90
  129.3 4.2 collective-permute-start.10
  136.2 3.0 collective-permute-start.9
  142.7 41.5 %all-reduce.29 = (f32[]{:T(128)}, f32[]{:T(128)}) all-reduce(f32[]{:T(128)} %get-tuple-element.37, f32[]{:T(128)} %get-tuple-element.36), channel_id=1, replica_groups=mesh['sec'=4,'tile'=8] {'sec','tile'}, use_global_device_ids=true, to_apply=%region_9.10 | all-reduce | flops 2 | bytes 16 | tf_op jit(solution)/shard_map/psum | solution.py:90
  187.1 4.2 collective-permute-start.14
  193.9 3.0 collective-permute-start.13
  200.4 42.6 %all-reduce.28 = (f32[]{:T(128)}, f32[]{:T(128)}) all-reduce(f32[]{:T(128)} %get-tuple-element.35, f32[]{:T(128)} %get-tuple-element.34), channel_id=1, replica_groups=mesh['sec'=4,'tile'=8] {'sec','tile'}, use_global_device_ids=true, to_apply=%region_13.14 | all-reduce | flops 2 | bytes 16 | tf_op jit(solution)/shard_map/psum | solution.py:90
  245.7 4.2 collective-permute-start.18
  252.5 3.0 collective-permute-start.17
  259.0 41.5 %all-reduce.27 = (f32[]{:T(128)}, f32[]{:T(128)}) all-reduce(f32[]{:T(128)} %get-tuple-element.33, f32[]{:T(128)} %get-tuple-element.32), channel_id=1, replica_groups=mesh['sec'=4,'tile'=8] {'sec','tile'}, use_global_device_ids=true, to_apply=%region_17.18 | all-reduce | flops 2 | bytes 16 | tf_op jit(solution)/shard_map/psum | solution.py:90
  303.4 4.2 collective-permute-start.22
  310.3 3.0 collective-permute-start.21
  316.8 42.6 %all-reduce.26 = (f32[]{:T(128)}, f32[]{:T(128)}) all-reduce(f32[]{:T(128)} %get-tuple-element.31, f32[]{:T(128)} %get-tuple-element.30), channel_id=1, replica_groups=mesh['sec'=4,'tile'=8] {'sec','tile'}, use_global_device_ids=true, to_apply=%region_21.22 | all-reduce | flops 2 | bytes 16 | tf_op jit(solution)/shard_map/psum | solution.py:90
  362.2 4.2 collective-permute-start.26
  369.0 3.0 collective-permute-start.25
  375.4 41.5 %all-reduce.25 = (f32[]{:T(128)}, f32[]{:T(128)}) all-reduce(f32[]{:T(128)} %get-tuple-element.29, f32[]{:T(128)} %get-tuple-element.28), channel_id=1, replica_groups=mesh['sec'=4,'tile'=8] {'sec','tile'}, use_global_device_ids=true, to_apply=%region_25.26 | all-reduce | flops 2 | bytes 16 | tf_op jit(solution)/shard_map/psum | solution.py:90
  419.6 4.2 collective-permute-start.30
  426.4 3.5 collective-permute-start.29
  433.0 42.6 %all-reduce.24 = (f32[]{:T(128)}, f32[]{:T(128)}) all-reduce(f32[]{:T(128)} %get-tuple-element.27, f32[]{:T(128)} %get-tuple-element.26), channel_id=1, replica_groups=mesh['sec'=4,'tile'=8] {'sec','tile'}, use_global_device_ids=true, to_apply=%region_29.30 | all-reduce | flops 2 | bytes 16 | tf_op jit(solution)/shard_map/psum | solution.py:90
  478.4 4.2 collective-permute-start.34
  485.2 3.0 collective-permute-start.33
  491.6 41.4 %all-reduce.23 = (f32[]{:T(128)}, f32[]{:T(128)}) all-reduce(f32[]{:T(128)} %get-tuple-element.25, f32[]{:T(128)} %get-tuple-element.24), channel_id=1, replica_groups=mesh['sec'=4,'tile'=8] {'sec','tile'}, use_global_device_ids=true, to_apply=%region_33.34 | all-reduce | flops 2 | bytes 16 | tf_op jit(solution)/shard_map/psum | solution.py:90
  535.7 4.2 collective-permute-start.38
  542.5 3.0 collective-permute-start.37
  547.3 2.3 multiply_reduce_fusion.12
  549.6 42.6 %all-reduce.22 = (f32[]{:T(128)}, f32[]{:T(128)}) all-reduce(f32[]{:T(128)} %get-tuple-element.23, f32[]{:T(128)} %get-tuple-element.22), channel_id=1, replica_groups=mesh['sec'=4,'tile'=8] {'sec','tile'}, use_global_device_ids=true, to_apply=%region_37.38 | all-reduce | flops 2 | bytes 16 | tf_op jit(solution)/shard_map/psum | solution.py:90
  595.8 4.2 collective-permute-start.42
  602.6 3.0 collective-permute-start.41
  606.5 3.5 all-to-all-start
  612.3 42.3 %all-reduce.21 = (f32[]{:T(128)}, f32[]{:T(128)}) all-reduce(f32[]{:T(128)} %get-tuple-element.21, f32[]{:T(128)} %get-tuple-element.20), channel_id=1, replica_groups=mesh['sec'=4,'tile'=8] {'sec','tile'}, use_global_device_ids=true, to_apply=%region_41.42 | all-reduce | flops 2 | bytes 16 | tf_op jit(solution)/shard_map/psum | solution.py:90
  657.4 4.2 collective-permute-start.46
  664.2 3.0 collective-permute-start.45
  670.8 42.6 %all-reduce.20 = (f32[]{:T(128)}, f32[]{:T(128)}) all-reduce(f32[]{:T(128)} %get-tuple-element.19, f32[]{:T(128)} %get-tuple-element.18), channel_id=1, replica_groups=mesh['sec'=4,'tile'=8] {'sec','tile'}, use_global_device_ids=true, to_apply=%region_45.46 | all-reduce | flops 2 | bytes 16 | tf_op jit(solution)/shard_map/psum | solution.py:90
  716.0 4.2 collective-permute-start.50
  722.8 3.0 collective-permute-start.49
  729.3 41.5 %all-reduce.19 = (f32[]{:T(128)}, f32[]{:T(128)}) all-reduce(f32[]{:T(128)} %get-tuple-element.17, f32[]{:T(128)} %get-tuple-element.16), channel_id=1, replica_groups=mesh['sec'=4,'tile'=8] {'sec','tile'}, use_global_device_ids=true, to_apply=%region_49.50 | all-reduce | flops 2 | bytes 16 | tf_op jit(solution)/shard_map/psum | solution.py:90
  773.7 4.2 collective-permute-start.54
  780.5 3.0 collective-permute-start.53
  787.0 42.6 %all-reduce.18 = (f32[]{:T(128)}, f32[]{:T(128)}) all-reduce(f32[]{:T(128)} %get-tuple-element.15, f32[]{:T(128)} %get-tuple-element.14), channel_id=1, replica_groups=mesh['sec'=4,'tile'=8] {'sec','tile'}, use_global_device_ids=true, to_apply=%region_53.54 | all-reduce | flops 2 | bytes 16 | tf_op jit(solution)/shard_map/psum | solution.py:90
  832.4 4.2 collective-permute-start.58
  839.2 3.0 collective-permute-start.57
  845.6 41.7 %all-reduce.17 = (f32[]{:T(128)}, f32[]{:T(128)}) all-reduce(f32[]{:T(128)} %get-tuple-element.13, f32[]{:T(128)} %get-tuple-element.12), channel_id=1, replica_groups=mesh['sec'=4,'tile'=8] {'sec','tile'}, use_global_device_ids=true, to_apply=%region_57.58 | all-reduce | flops 2 | bytes 16 | tf_op jit(solution)/shard_map/psum | solution.py:90
  889.9 4.2 collective-permute-start.62
  896.7 3.0 collective-permute-start.61
  903.2 42.6 %all-reduce.16 = (f32[]{:T(128)}, f32[]{:T(128)}) all-reduce(f32[]{:T(128)} %get-tuple-element.11, f32[]{:T(128)} %get-tuple-element.10), channel_id=1, replica_groups=mesh['sec'=4,'tile'=8] {'sec','tile'}, use_global_device_ids=true, to_apply=%region_61.62 | all-reduce | flops 2 | bytes 16 | tf_op jit(solution)/shard_map/psum | solution.py:90
  948.4 8.5 copy.33
  956.9 6.3 gather_fusion
  964.3 3.5 all-to-all-start.1
  967.9 4.3 fusion.20
  972.2 3.3 copy.36
  975.5 5.1 all-to-all-start.2
  981.0 93.7 %all-to-all-done.2 = f32[8,2,256,256]{3,2,1,0:T(8,128)} async-done(((f32[8,2,256,256]{3,2,1,0:T(8,128)}), f32[8,2,256,256]{3,2,1,0:T(8,128)}, u32[]{:S(2)}, u32[]{:S(2)}) %all-to-all-start.2) | async-done | bytes 4194336 | tf_op jit(solution)/shard_map/all_to_all | solution.py:124
  1074.7 10.5 fusion.2
  1085.2 12.1 %fusion.7 = f32[16,384,384]{2,1,0:T(8,128)S(1)} fusion(f32[16,256,384]{2,1,0:T(8,128)S(1)} %fusion.2, f32[16]{0:T(128)S(1)} %sub.587, f32[384,256]{1,0:T(8,128)S(1)} %broadcast_subtract_fusion), kind=kOutput, calls=%fused_computation.8 | convolution fusion | flops 7254048768 | bytes 16121920 | tf_op jit(solution)/shard_map/bri,bik->brk/dot_general | solution.py:62
  1097.3 11.2 %fusion.23 = f32[2,384,384]{2,0,1:T(2,128)S(1)} fusion(f32[8,2,384,384]{3,2,1,0:T(8,128)S(1)} %bitcast.214, f32[8,2,2]{0,2,1:T(2,128)S(1)} %copy.37), kind=kOutput, calls=%fused_computation.24 | convolution fusion | flops 56623104 | bytes 10616960 | tf_op jit(solution)/shard_map/skc,skrq->kcrq/dot_general | solution.py:135
  (204 shorter events, 98.7 us)
Async XLA Ops:
  1.8 12.1 %collective-permute-start.2 = (f32[2,2,32,256]{3,2,1,0:T(8,128)S(1)}, f32[2,2,32,256]{3,2,1,0:T(8,128)S(1)}, u32[]{:S(2)}, u32[]{:S(2)}) collective-permute-start(f32[2,2,32,256]{3,2,1,0:T(8,128)S(1)} %get-tuple-element.205), channel_id=1, source_target_pairs={{0,8},{8,16},{16,24},{1,9},{9,17},{17,25},{2,10},{10,18},{18,26},{... | collective-permute-start | bytes 393224 | tf_op jit(solution)/shard_map/ppermute | solution.py:27
  6.6 12.6 %collective-permute-start.3 = (f32[2,2,32,256]{3,2,1,0:T(8,128)S(1)}, f32[2,2,32,256]{3,2,1,0:T(8,128)S(1)}, u32[]{:S(2)}, u32[]{:S(2)}) collective-permute-start(f32[2,2,32,256]{3,2,1,0:T(8,128)S(1)} %get-tuple-element.206), channel_id=1, source_target_pairs={{8,0},{16,8},{24,16},{9,1},{17,9},{25,17},{10,2},{18,10},{26,18},{... | collective-permute-start | bytes 393224 | tf_op jit(solution)/shard_map/ppermute | solution.py:28
  14.9 4.4 collective-permute-start
  16.2 3.8 collective-permute-start.1
  69.4 10.7 collective-permute-start.6
  73.6 7.4 collective-permute-start.7
  74.9 5.0 collective-permute-start.4
  76.2 3.8 collective-permute-start.5
  129.3 10.7 collective-permute-start.10
  133.5 7.4 collective-permute-start.11
  134.9 5.0 collective-permute-start.8
  136.2 3.8 collective-permute-start.9
  187.1 10.7 collective-permute-start.14
  191.3 7.5 collective-permute-start.15
  192.6 5.0 collective-permute-start.12
  193.9 3.8 collective-permute-start.13
  245.7 10.7 collective-permute-start.18
  249.9 7.4 collective-permute-start.19
  251.2 5.0 collective-permute-start.16
  252.5 3.8 collective-permute-start.17
  303.4 10.7 collective-permute-start.22
  307.6 7.5 collective-permute-start.23
  309.0 5.0 collective-permute-start.20
  310.3 3.8 collective-permute-start.21
  362.2 10.7 collective-permute-start.26
  366.4 7.5 collective-permute-start.27
  367.7 5.1 collective-permute-start.24
  369.0 3.9 collective-permute-start.25
  419.6 11.1 collective-permute-start.30
  423.8 7.4 collective-permute-start.31
  425.1 5.5 collective-permute-start.28
  426.4 4.3 collective-permute-start.29
  478.4 11.2 %collective-permute-start.34 = (f32[2,2,32,256]{3,2,1,0:T(8,128)S(1)}, f32[2,2,32,256]{3,2,1,0:T(8,128)S(1)}, u32[]{:S(2)}, u32[]{:S(2)}) collective-permute-start(f32[2,2,32,256]{3,2,1,0:T(8,128)S(1)} %get-tuple-element.172), channel_id=1, source_target_pairs={{0,8},{8,16},{16,24},{1,9},{9,17},{17,25},{2,10},{10,18},{18,26},{... | collective-permute-start | bytes 393224 | tf_op jit(solution)/shard_map/ppermute | solution.py:27
  482.6 7.4 collective-permute-start.35
  483.9 5.6 collective-permute-start.32
  485.2 4.3 collective-permute-start.33
  535.7 10.7 collective-permute-start.38
  539.9 7.4 collective-permute-start.39
  541.2 4.9 collective-permute-start.36
  542.5 3.8 collective-permute-start.37
  595.8 14.8 %collective-permute-start.42 = (f32[2,2,32,256]{3,2,1,0:T(8,128)S(1)}, f32[2,2,32,256]{3,2,1,0:T(8,128)S(1)}, u32[]{:S(2)}, u32[]{:S(2)}) collective-permute-start(f32[2,2,32,256]{3,2,1,0:T(8,128)S(1)} %get-tuple-element.164), channel_id=1, source_target_pairs={{0,8},{8,16},{16,24},{1,9},{9,17},{17,25},{2,10},{10,18},{18,26},{... | collective-permute-start | bytes 393224 | tf_op jit(solution)/shard_map/ppermute | solution.py:27
  600.0 10.6 collective-permute-start.43
  601.3 9.3 collective-permute-start.40
  602.6 8.0 collective-permute-start.41
  606.5 357.9 %all-to-all-start = ((f32[8,2,2]{2,1,0:T(2,128)}), f32[8,2,2]{2,1,0:T(2,128)S(1)}, u32[]{:S(2)}, u32[]{:S(2)}) async-start(f32[8,2,2]{2,1,0:T(2,128)} %bitcast.43), calls=%async_computation | async-start | bytes 16384 | tf_op jit(solution)/shard_map/all_to_all | solution.py:126
  657.4 10.7 collective-permute-start.46
  661.6 7.4 collective-permute-start.47
  662.9 5.0 collective-permute-start.44
  664.2 3.8 collective-permute-start.45
  716.0 10.7 collective-permute-start.50
  720.2 7.4 collective-permute-start.51
  721.5 4.9 collective-permute-start.48
  722.8 3.8 collective-permute-start.49
  773.7 10.7 collective-permute-start.54
  777.9 7.4 collective-permute-start.55
  779.2 5.0 collective-permute-start.52
  832.4 10.7 collective-permute-start.58
  836.6 7.4 collective-permute-start.59
  837.9 5.0 collective-permute-start.56
  889.9 10.7 collective-permute-start.62
  894.1 7.4 collective-permute-start.63
  895.4 5.0 collective-permute-start.60
  964.3 11.1 %all-to-all-start.1 = ((f32[8,2,2]{1,2,0:T(2,128)}), f32[8,2,2]{1,2,0:T(2,128)S(1)}, u32[]{:S(2)}, u32[]{:S(2)}) async-start(f32[8,2,2]{1,2,0:T(2,128)} %copy.34), calls=%async_computation.1 | async-start | bytes 16384 | tf_op jit(solution)/shard_map/all_to_all | solution.py:125
  975.5 99.2 %all-to-all-start.2 = ((f32[8,2,256,256]{3,2,1,0:T(8,128)}), f32[8,2,256,256]{3,2,1,0:T(8,128)}, u32[]{:S(2)}, u32[]{:S(2)}) async-start(f32[8,2,256,256]{3,2,1,0:T(8,128)} %copy.36), calls=%async_computation.2 | async-start | bytes 8388608 | tf_op jit(solution)/shard_map/all_to_all | solution.py:124
  (10 other events, 775.3 us)
where the time goes:
time: 1120 us; the launch traced here: 1110 us
  blocking collectives  676 us (60%)
  starting transfers between devices  170 us (15%)
  waiting for transfers between devices  109 us (10%)
  other arithmetic  45.2 us (4%)
  between operations  45.2 us (4%)
  matrix products  39 us (3%)
  local copies, waits for them, and re-layouts  26 us (2%)
    psum x16, blocking collectives, body(): lax.psum((jnp.sum(velocity * velocity), jnp.sum(push * push)), ('sec', 't...  676 us
    ppermute x32, starting transfers between devices, with_halo(): before = lax.ppermute(last, axis, up)  117 us
    all_to_all x1, waiting for transfers between devices, body(): lax.all_to_all(send_blocks, 'tile', split_axis=0, concat_axis=0, tiled=True)  93.7 us
    ppermute x32, starting transfers between devices, with_halo(): after = lax.ppermute(leading, axis, down)  41.3 us
    reduce_sum x16, other arithmetic, body(): jnp.sum(push * push)  29.4 us
  transfers between devices with their start and end apart: 67, of which 27 were waited for; matrix products, arithmetic and copies ran while one was open for 4% of the time, Pallas kernels for 0%

commit v1 on v0

v1 whole, which is shorter than its diff:
```python
import functools

import jax
import jax.numpy as jnp
from jax import lax
from jax.experimental import pallas as pl
from jax.experimental.pallas import tpu as pltpu
from jax.sharding import PartitionSpec as P


OUTER = 2
FIRE_STEPS = 8
CH = 384
SPAN_DEV = 2
REACHES = (-2, -1, 1, 2)

MIXING = 0.1
EPSILON = 1e-06
SPEED_CAP = 0.1
HALF = 8.0
MESH = pl.DeviceIdType.MESH
LANES = 128


def pair_order(index):
    odd = (index // 2) % 2
    return index + odd * (1 - 2 * (index % 2))


def fire_kernel(
    n_sec, n_tile, steps, keep, packed, out,
    fields, disp, basis, diag, edge_up, edge_dn, halo_up, halo_dn, rows, gram, from_sec, from_tile,
    in_send, in_recv, up_send, up_recv, dn_send, dn_recv,
    gs_send, gs_recv, gt_send, gt_recv, out_send, out_recv,
):
    s, t = lax.axis_index("sec"), lax.axis_index("tile")
    own, n_rows, width = packed.shape[1], packed.shape[3], packed.shape[4]
    sections = own * n_sec
    node_total = float(2 * sections * width * width)

    def place(which, tile):
        order = pair_order(which)
        return order + (tile % 2) * (n_sec - 1 - 2 * order)

    q = place(s, t)
    first = jnp.logical_and(q == 0, t == 0)
    last = jnp.logical_and(q == n_sec - 1, t == n_tile - 1)

    def holder(position):
        tile = position // n_sec
        at = position % n_sec
        return pair_order(at + (tile % 2) * (n_sec - 1 - 2 * at)), tile

    position = t * n_sec + q
    above = holder(lax.rem(position - 1 + n_sec * n_tile, n_sec * n_tile))
    below = holder(lax.rem(position + 1, n_sec * n_tile))

    barrier = pltpu.get_barrier_semaphore()
    for j in range(1, n_sec):
        pl.semaphore_signal(barrier, inc=1, device_id=(lax.rem(s + j, n_sec), t), device_id_type=MESH)
    for j in range(1, n_tile):
        pl.semaphore_signal(barrier, inc=1, device_id=(s, lax.rem(t + j, n_tile)), device_id_type=MESH)
    pl.semaphore_wait(barrier, n_sec + n_tile - 2)

    def send_in(j):
        peer = lax.rem(s + j, n_sec)
        return pltpu.make_async_remote_copy(
            src_ref=packed.at[:, :, place(peer, t)], dst_ref=fields.at[:, pl.ds(s * own, own)],
            send_sem=in_send.at[j], recv_sem=in_recv.at[j], device_id=(peer, t), device_id_type=MESH)

    for j in range(1, n_sec):
        send_in(j).start()
    mine = pltpu.make_async_copy(packed.at[:, :, q], fields.at[:, pl.ds(s * own, own)], in_recv.at[0])
    mine.start()
    blank = jnp.zeros((n_rows, width), jnp.float32)
    for c in range(2):
        for i in (0, 1, sections + 2, sections + 3):
            disp[c, i] = blank
            for k in range(FIRE_STEPS + 1):
                basis[k, c, i] = blank
        for i in range(sections):
            basis[0, c, i + 2] = blank

    @pl.when(first)
    def _():
        halo_up[...] = jnp.zeros_like(halo_up)

    @pl.when(last)
    def _():
        halo_dn[...] = jnp.zeros_like(halo_dn)

    rows[...] = jnp.zeros_like(rows)
    mine.wait()
    for j in range(1, n_sec):
        send_in(j).wait()

    for i in range(sections):
        diag[i] = 4.0 + fields[0, i] + fields[1, i] + fields[2, i] + fields[3, i]
        for c in range(2):
            disp[c, i + 2] = fields[6 + c, i]

    column = lax.broadcasted_iota(jnp.int32, (n_rows, width), 1)
    sub = lax.broadcasted_iota(jnp.int32, (8, LANES), 0)
    lane = lax.broadcasted_iota(jnp.int32, (8, LANES), 1)

    def to_up(k):
        return pltpu.make_async_remote_copy(
            src_ref=edge_up.at[k], dst_ref=halo_dn.at[k],
            send_sem=up_send.at[k], recv_sem=up_recv.at[k], device_id=above, device_id_type=MESH)

    def to_dn(k):
        return pltpu.make_async_remote_copy(
            src_ref=edge_dn.at[k], dst_ref=halo_up.at[k],
            send_sem=dn_send.at[k], recv_sem=dn_recv.at[k], device_id=below, device_id_type=MESH)

    def all_sum(outer):
        def over(j, axis):
            if axis == 0:
                peer, land, send, recv = (lax.rem(s + j, n_sec), t), from_sec, gs_send, gs_recv
            else:
                peer, land, send, recv = (s, lax.rem(t + j, n_tile)), from_tile, gt_send, gt_recv
            return pltpu.make_async_remote_copy(
                src_ref=gram.at[outer, axis], dst_ref=land.at[outer, j],
                send_sem=send.at[outer, j], recv_sem=recv.at[outer, j], device_id=peer, device_id_type=MESH)

        total = gram[outer, 0]
        for axis, size, land in ((0, n_sec, from_sec), (1, n_tile, from_tile)):
            if axis == 1:
                gram[outer, 1] = total
            for j in range(1, size):
                over(j, axis).start()
            for j in range(1, size):
                over(j, axis).wait()
            for j in range(1, size):
                total = total + land[outer, j]
        return total

    for outer in range(OUTER):
        for c in range(2):
            for i in range(sections):
                here = disp[c, i + 2]
                push = fields[4 + c, i]
                for which, reach in enumerate(REACHES):
                    push = push + fields[which, i] * (disp[c, i + 2 + reach] - here)
                basis[1, c, i + 2] = push

        def apply(k, carry):
            for c in range(2):
                edge_up[k, c] = basis[k + 1, c, pl.ds(2, sections), 0, :]
                edge_dn[k, c] = basis[k + 1, c, pl.ds(2, sections), n_rows - 1, :]

            @pl.when(jnp.logical_not(first))
            def _():
                to_up(k).start()

            @pl.when(jnp.logical_not(last))
            def _():
                to_dn(k).start()

            @pl.when(jnp.logical_not(first))
            def _():
                to_up(k).wait_send()
                to_dn(k).wait_recv()

            @pl.when(jnp.logical_not(last))
            def _():
                to_dn(k).wait_send()
                to_up(k).wait_recv()

            twice = jnp.where(k == 0, 1.0, 2.0)
            for c in range(2):
                for i in range(sections):
                    x = basis[k + 1, c, i + 2]
                    higher = jnp.concatenate([halo_up[k, c, i : i + 1, :], x[: n_rows - 1]], axis=0)
                    lower = jnp.concatenate([x[1:], halo_dn[k, c, i : i + 1, :]], axis=0)
                    left = jnp.where(column == 0, 0.0, pltpu.roll(x, 1, 1))
                    right = jnp.where(column == width - 1, 0.0, pltpu.roll(x, width - 1, 1))
                    summed = (higher + lower) + (left + right) - diag[i] * x
                    for which, reach in enumerate(REACHES):
                        summed = summed + fields[which, i] * basis[k + 1, c, i + 2 + reach]
                    basis[k + 2, c, i + 2] = twice * (summed * (1.0 / HALF) + x) - basis[k, c, i + 2]
            return carry

        lax.fori_loop(0, FIRE_STEPS - 1, apply, 0)

        pairs = [(j, k) for j in range(FIRE_STEPS) for k in range(j, FIRE_STEPS)]

        def products(i, carry):
            for c in range(2):
                for part in range(width // LANES):
                    own_k = [basis[k + 1, c, i + 2, :, part * LANES : (part + 1) * LANES] for k in range(FIRE_STEPS)]
                    carry = tuple(a + own_k[j] * own_k[k] for a, (j, k) in zip(carry, pairs))
            return carry

        zero = jnp.zeros((n_rows, LANES), jnp.float32)
        sums = lax.fori_loop(0, sections, products, tuple(zero for _ in pairs))
        for value, (j, k) in zip(sums, pairs):
            line = jnp.sum(value, axis=0, keepdims=True)
            rows[8 * j + k : 8 * j + k + 1, :] = line
            if j != k:
                rows[8 * k + j : 8 * k + j + 1, :] = line
        dots = jnp.sum(rows[...], axis=1, keepdims=True)
        local = jnp.zeros((8, LANES), jnp.float32)
        for j in range(FIRE_STEPS):
            local = jnp.where(lane == j, dots[8 * j : 8 * j + 8], local)
        gram[outer, 0] = local
        matrix = all_sum(outer)

        def force_row(v):
            before = jnp.where(lane == 0, 0.0, pltpu.roll(v, 1, 1))
            after = jnp.where(lane == LANES - 1, 0.0, pltpu.roll(v, LANES - 1, 1))
            return HALF * (0.5 * (before + after) + jnp.where(lane == 1, 0.5 * before, 0.0) - v)

        def force_col(v):
            before = jnp.where(sub == 0, 0.0, pltpu.roll(v, 1, 0))
            after = jnp.where(sub == 7, 0.0, pltpu.roll(v, 7, 0))
            return HALF * (0.5 * (before + after) + jnp.where(sub == 1, 0.5 * before, 0.0) - v)

        def square(row, col):
            parts = jnp.sum(matrix * row * col, axis=1, keepdims=True)
            return jnp.maximum(jnp.sum(parts, axis=0, keepdims=True), 0.0)

        f_row, f_col = (lane == 0).astype(jnp.float32), (sub == 0).astype(jnp.float32)
        v_row, v_col = jnp.zeros_like(f_row), jnp.zeros_like(f_row)
        gain = jnp.zeros_like(f_row)
        for step in range(FIRE_STEPS):
            h = steps[outer, step]
            v_row, v_col = v_row + h * f_row, v_col + h * f_col
            vv, ff = square(v_row, v_col), square(f_row, f_col)
            ratio = jnp.sqrt(vv + EPSILON) / jnp.sqrt(ff + EPSILON)
            limit = jnp.minimum(1.0, SPEED_CAP / jnp.sqrt(vv * (1.0 / node_total) + EPSILON))
            scale = limit * keep[outer, step]
            mix = MIXING * ratio
            v_row = scale * ((1.0 - MIXING) * v_row + mix * f_row)
            v_col = scale * ((1.0 - MIXING) * v_col + mix * f_col)
            gain = gain + h * v_col
            if step < FIRE_STEPS - 1:
                f_row, f_col = f_row + h * force_row(v_row), f_col + h * force_col(v_col)
        wide = [
            jnp.broadcast_to(jnp.concatenate([gain[k : k + 1]] * (width // LANES), axis=1), (n_rows, width))
            for k in range(FIRE_STEPS)
        ]
        for c in range(2):
            for i in range(sections):
                moved = disp[c, i + 2]
                for k in range(FIRE_STEPS):
                    moved = moved + wide[k] * basis[k + 1, c, i + 2]
                disp[c, i + 2] = moved

    def send_out(j):
        peer = lax.rem(s + j, n_sec)
        return pltpu.make_async_remote_copy(
            src_ref=disp.at[:, pl.ds(2 + peer * own, own)], dst_ref=out.at[:, :, q],
            send_sem=out_send.at[j], recv_sem=out_recv.at[j], device_id=(peer, t), device_id_type=MESH)

    for j in range(1, n_sec):
        send_out(j).start()
    mine = pltpu.make_async_copy(disp.at[:, pl.ds(2 + s * own, own)], out.at[:, :, q], out_recv.at[0])
    mine.start()
    mine.wait()
    for j in range(1, n_sec):
        send_out(j).wait()


def relax(packed, steps, keep, n_sec, n_tile):
    _, own, _, n_rows, width = packed.shape
    sections = own * n_sec
    f32 = jnp.float32
    dma = pltpu.SemaphoreType.DMA
    vmem = pl.BlockSpec(memory_space=pltpu.VMEM)
    smem = pl.BlockSpec(memory_space=pltpu.SMEM)
    hops = FIRE_STEPS - 1
    edges = pltpu.VMEM((hops, 2, sections, width), f32)
    return pl.pallas_call(
        functools.partial(fire_kernel, n_sec, n_tile),
        out_shape=jax.ShapeDtypeStruct((2,) + packed.shape[1:], f32),
        in_specs=[smem, smem, vmem],
        out_specs=vmem,
        scratch_shapes=[
            pltpu.VMEM((8, sections, n_rows, width), f32),
            pltpu.VMEM((2, sections + 4, n_rows, width), f32),
            pltpu.VMEM((FIRE_STEPS + 1, 2, sections + 4, n_rows, width), f32),
            pltpu.VMEM((sections, n_rows, width), f32),
            edges, edges, edges, edges,
            pltpu.VMEM((64, LANES), f32),
            pltpu.VMEM((OUTER, 2, 8, LANES), f32),
            pltpu.VMEM((OUTER, n_sec, 8, LANES), f32),
            pltpu.VMEM((OUTER, n_tile, 8, LANES), f32),
            dma((n_sec,)), dma((n_sec,)),
            dma((hops,)), dma((hops,)), dma((hops,)), dma((hops,)),
            dma((OUTER, n_sec)), dma((OUTER, n_sec)), dma((OUTER, n_tile)), dma((OUTER, n_tile)),
            dma((n_sec,)), dma((n_sec,)),
        ],
        compiler_params=pltpu.CompilerParams(collective_id=0, has_side_effects=True),
        cost_estimate=pl.CostEstimate(flops=10**9, bytes_accessed=2 * 10**8, transcendentals=0),
        name="relax",
    )(steps, keep, packed)


def copy_block(index, source, target):
    target[...] = source[...]


def place_blocks(blocks, index):
    count = index.shape[0]
    side = blocks.shape[1:]
    return pl.pallas_call(
        copy_block,
        grid_spec=pltpu.PrefetchScalarGridSpec(
            num_scalar_prefetch=1, grid=(count,),
            in_specs=[pl.BlockSpec((1,) + side, lambda i, at: (at[i], 0, 0))],
            out_specs=pl.BlockSpec((1,) + side, lambda i, at: (i, 0, 0)),
        ),
        out_shape=jax.ShapeDtypeStruct((count,) + side, jnp.float32),
        name="place",
    )(index, blocks)


def pick_kernel(anchor, source, target):
    lane = lax.broadcasted_iota(jnp.int32, (1, source.shape[2]), 1)
    for b in range(target.shape[1]):
        node = anchor[b]
        for c in range(2):
            line = source[c, pl.ds(node // source.shape[2], 1), :]
            value = jnp.sum(jnp.where(lane == node % source.shape[2], line, 0.0), axis=1, keepdims=True)
            target[c, b : b + 1, :] = jnp.broadcast_to(value, (1, LANES))


def pick_nodes(field, anchor):
    return pl.pallas_call(
        pick_kernel,
        out_shape=jax.ShapeDtypeStruct((2, anchor.shape[0], LANES), jnp.float32),
        in_specs=[pl.BlockSpec(memory_space=pltpu.SMEM), pl.BlockSpec(memory_space=pltpu.VMEM)],
        out_specs=pl.BlockSpec(memory_space=pltpu.VMEM),
        name="pick",
    )(anchor, field)[:, :, 0]


def split_dot(a, b, dims):
    a_hi, b_hi = a.astype(jnp.bfloat16), b.astype(jnp.bfloat16)
    a_lo = (a - a_hi.astype(jnp.float32)).astype(jnp.bfloat16)
    b_lo = (b - b_hi.astype(jnp.float32)).astype(jnp.bfloat16)
    dot = functools.partial(lax.dot_general, dimension_numbers=dims, preferred_element_type=jnp.float32)
    return dot(a_hi, b_hi) + (dot(a_hi, b_lo) + dot(a_lo, b_hi))


def render_kernel(slot, shift, blocks, spans):
    item = pl.program_id(0)

    @pl.when(item == 0)
    def _():
        spans[...] = jnp.zeros_like(spans)

    chosen = slot[item]

    @pl.when(chosen >= 0)
    def _():
        side, size = blocks.shape[1], spans.shape[1]
        y, x = shift[2 * item], shift[2 * item + 1]
        out_at = lax.broadcasted_iota(jnp.int32, (size, side), 0)
        in_at = lax.broadcasted_iota(jnp.int32, (size, side), 1)
        apart = (out_at - in_at).astype(jnp.float32)
        row_hats = jnp.maximum(0.0, 1.0 - jnp.abs(apart - y))
        col_hats = jnp.maximum(0.0, 1.0 - jnp.abs(apart - x))
        halfway = split_dot(blocks[0], col_hats, (((1,), (1,)), ((), ())))
        drawn = split_dot(row_hats, halfway, (((1,), (0,)), ((), ())))
        spans[chosen] = spans[chosen] + drawn


def render(blocks, slot, shift):
    count, side, _ = blocks.shape
    return pl.pallas_call(
        render_kernel,
        grid_spec=pltpu.PrefetchScalarGridSpec(
            num_scalar_prefetch=2, grid=(count,),
            in_specs=[pl.BlockSpec((1, side, side), lambda i, *_: (i, 0, 0))],
            out_specs=pl.BlockSpec((SPAN_DEV, CH, CH), lambda i, *_: (0, 0, 0)),
        ),
        out_shape=jax.ShapeDtypeStruct((SPAN_DEV, CH, CH), jnp.float32),
        name="render",
    )(slot, shift, blocks)


def body(
    n_sec, n_tile,
    displacement, coupling, matches, step_sizes, restarts, images,
    block_anchor, block_dest, block_slot, block_offset, block_count,
):
    own, tile_rows, width = displacement.shape[1:]
    tiles = n_tile

    blocks_here = block_anchor.shape[1]
    owners = block_dest[0, :, 0]
    capacity = max(2, 2 * blocks_here // tiles)
    owner_hot = (owners[:, None] == jnp.arange(tiles)[None, :]).astype(jnp.int32)
    rank_all = jnp.cumsum(owner_hot, axis=0) - owner_hot
    position = owners * capacity + jnp.sum(rank_all * owner_hot, axis=1)
    placer = position[None, :] == jnp.arange(tiles * capacity)[:, None]
    held = jnp.arange(blocks_here, dtype=jnp.int32)
    block_of = jnp.sum(jnp.where(placer, held[None, :], 0), axis=1)
    send_blocks = place_blocks(images[0], block_of)
    blocks_in = lax.all_to_all(send_blocks, "tile", split_axis=0, concat_axis=0, tiled=True)

    section = lax.axis_index("sec") * own + jnp.arange(own)
    reach = jnp.array(REACHES, jnp.int32)[:, None]
    valid = (section[None] + reach >= 0) & (section[None] + reach < own * n_sec)
    springs = jnp.where(valid[:, :, None, None], coupling, 0.0)
    pull = jnp.sum(springs[:, None] * matches, axis=0)
    packed = jnp.concatenate([springs, pull, displacement], axis=0)
    packed = packed.reshape(8, own, n_sec, tile_rows // n_sec, width)
    keep = 1.0 - restarts.astype(jnp.float32)
    aligned = relax(packed, step_sizes, keep, n_sec, n_tile)
    aligned = aligned.reshape(displacement.shape)

    moved = pick_nodes(aligned.reshape(2, own * tile_rows, width), block_anchor[0])
    shifts = block_offset[0].astype(jnp.float32) + moved.T
    target = jnp.where(held < block_count[0, 0], block_slot[0] + 1, 0).astype(jnp.float32)
    small = jnp.concatenate([shifts, target[:, None], jnp.zeros_like(target)[:, None]], axis=1)
    send_small = jnp.sum(jnp.where(placer[:, :, None], small[None], 0.0), axis=1)
    send_small, blocks_in = lax.optimization_barrier((send_small, blocks_in))
    small_in = lax.all_to_all(send_small, "tile", split_axis=0, concat_axis=0, tiled=True)
    slot = small_in[:, 2].astype(jnp.int32) - 1
    spans = render(blocks_in, slot, small_in[:, :2].reshape(-1))
    return (aligned, spans)


def solution(mesh):
    placed = (
        P(None, "sec", "tile", None),
        P(None, "sec", "tile", None),
        P(None, None, "sec", "tile", None),
        P(),
        P(),
        P("sec", "tile", None, None),
        P("sec", "tile"),
        P("sec", "tile", None),
        P("sec", "tile"),
        P("sec", "tile", None),
        P("sec", "tile"),
    )
    return jax.shard_map(
        functools.partial(body, mesh.shape["sec"], mesh.shape["tile"]),
        mesh=mesh,
        in_specs=placed,
        out_specs=(P(None, "sec", "tile", None), P(("sec", "tile"), None, None)),
        check_vma=False,
    )
```

time: 1120 us -> 211 us (0.19)
  blocking collectives: 676 us -> 0 us
  Pallas kernels: 0 us -> 185 us
  starting transfers between devices: 170 us -> 9.85 us
  waiting for transfers between devices: 109 us -> 5.61 us
  between operations: 45.2 us -> 1.38 us
  other arithmetic: 45.2 us -> 5.69 us
  matrix products: 39 us -> 0 us
  local copies, waits for them, and re-layouts: 26 us -> 2.89 us
    psum x16 -> x0, blocking collectives: 676 us -> none  [body(): lax.psum((jnp.sum(velocity * velocity), jnp.sum(push * push)), ('sec', 't...]
    pallas_call x0 -> x4, Pallas kernels: none -> 185 us  [the longest x1 157 us: relax(): pl.pallas_call(functools.partial(fire_kernel, n_sec, n_tile), out_shape=j...]
    ppermute x64 -> x0, starting transfers between devices: 158 us -> none  [the longest x32 117 us: with_halo(): before = lax.ppermute(last, axis, up)]
    all_to_all x1, waiting for transfers between devices: 93.7 us -> 0.01 us  [body(): lax.all_to_all(send_blocks, 'tile', split_axis=0, concat_axis=0, tiled=True)]
    dot_general x5 -> x0, matrix products: 38.2 us -> none  [the longest x1 12.1 us: warp_blocks(): return jnp.einsum('bri,bik->brk', row_hats, halfway, precision=PRECISE)]
    reduce_sum x17 -> x4, other arithmetic: 29.6 us -> 1.64 us  [the longest x1 0.84 us: body(): position = owners * capacity + jnp.sum(rank_all * owner_hot, axis=1)]
    ppermute x64 -> x0, waiting for transfers between devices: 15 us -> none  [the longest x32 12.3 us: with_halo(): after = lax.ppermute(leading, axis, down)]
  transfers between devices with their start and end apart: 67 -> 2, of which waited for: 27 -> 1; matrix products, arithmetic and copies ran while one was open for 4% -> 1% of each run, Pallas kernels for 0% -> 75%
where the time goes in v1:
time: 211 us; the launch traced here: 210 us
  Pallas kernels  185 us (88%)
  starting transfers between devices  9.85 us (5%)
  other arithmetic  5.69 us (3%)
  waiting for transfers between devices  5.61 us (3%)
  local copies, waits for them, and re-layouts  2.89 us (1%)
    pallas_call x1, Pallas kernels, relax(): pl.pallas_call(functools.partial(fire_kernel, n_sec, n_tile), out_shape=j...  157 us
    pallas_call x1, Pallas kernels, render(): pl.pallas_call(render_kernel, grid_spec=pltpu.PrefetchScalarGridSpec(num_...  15.7 us
    pallas_call x1, Pallas kernels, place_blocks(): pl.pallas_call(copy_block, grid_spec=pltpu.PrefetchScalarGridSpec(num_sca...  10.5 us
    all_to_all x1, starting transfers between devices, body(): lax.all_to_all(send_blocks, 'tile', split_axis=0, concat_axis=0, tiled=True)  6.44 us
    all_to_all x1, waiting for transfers between devices, body(): lax.all_to_all(send_small, 'tile', split_axis=0, concat_axis=0, tiled=True)  5.61 us
  transfers between devices with their start and end apart: 2, of which 1 were waited for; matrix products, arithmetic and copies ran while one was open for 1% of the time, Pallas kernels for 75%

profile of v1, /device:TPU:0, one launch (start us, length us, event | category | flops | bytes accessed | tf_op | source)
XLA Modules:
  0.0 210.2 jit_solution(11873205216097046223)
XLA Ops:
  0.6 0.7 fusion.2
  1.4 0.8 select_reduce_fusion.2
  2.2 0.7 multiply_add_fusion
  2.9 0.6 select_reduce_fusion.1.index
  3.5 10.5 %place.1 = f32[16,256,256]{2,1,0:T(8,128)} custom-call(s32[16]{0:T(128)} %select_reduce_fusion.1.index, f32[8,256,256]{2,1,0:T(8,128)} %bitcast.20), custom_call_target="tpu_custom_call" | custom-call | tf_op jit(solution)/shard_map/place/pallas_call | solution.py:307
  14.0 0.0 copy-start.7
  14.0 0.0 copy-start.2
  14.0 0.0 copy-start
  14.0 0.0 copy-start.3
  14.0 6.4 %all-to-all-start = ((f32[16,256,256]{2,1,0:T(8,128)}), f32[16,256,256]{2,1,0:T(8,128)}, u32[]{:S(2)}, u32[]{:S(2)}) async-start(f32[16,256,256]{2,1,0:T(8,128)} %place.1), calls=%async_computation | async-start | bytes 8388608 | tf_op jit(solution)/shard_map/all_to_all | solution.py:402
  20.4 0.0 copy-start.5
  21.1 0.1 pad.2.clone
  21.2 0.0 copy-done.7
  21.2 0.1 fusion.3
  21.3 0.0 copy-done.2
  21.3 0.1 broadcast_select_fusion
  21.4 0.0 copy-done
  21.4 0.0 copy-start.6
  21.4 0.0 copy-start.4
  21.4 0.1 multiply_reduce_fusion
  21.5 0.0 copy-done.3
  21.5 1.0 maximum_bitcast_fusion.packed
  22.6 0.0 copy-done.5
  22.6 0.6 convert_subtract_fusion.keep
  23.2 156.8 %relax.1 = f32[2,4,4,8,256]{4,3,2,1,0:T(8,128)} custom-call(f32[2,8]{1,0:T(2,128)} %steps.1, f32[2,8]{1,0:T(2,128)} %convert_subtract_fusion.keep, f32[8,4,4,8,256]{4,3,2,1,0:T(8,128)} %maximum_bitcast_fusion.packed), custom_call_target="tpu_custom_call" | custom-call | flops 1000000000 | bytes 200000000 | tf_op jit(solution)/shard_map/relax/pallas_call | solution.py:274
  180.0 0.0 copy-start.1
  180.0 1.8 pick.1
  181.7 0.8 slice_reduce_fusion
  182.5 0.0 copy-done.6
  182.5 0.1 iota_compare_fusion
  182.6 0.0 copy-done.4
  182.6 0.1 maximum_maximum_fusion
  182.7 0.1 select_reduce_fusion
  182.8 0.0 all-to-all-done.blocks
  182.8 0.7 copy.16
  183.4 3.4 %all-to-all-start.1 = ((f32[8,2,4]{2,1,0:T(2,128)}), f32[8,2,4]{2,1,0:T(2,128)S(1)}, u32[]{:S(2)}, u32[]{:S(2)}) async-start(f32[8,2,4]{2,1,0:T(2,128)} %bitcast.10), calls=%async_computation.1 | async-start | bytes 16384 | tf_op jit(solution)/shard_map/all_to_all | solution.py:421
  186.9 5.6 %all-to-all-done.1 = f32[8,2,4]{2,1,0:T(2,128)S(1)} async-done(((f32[8,2,4]{2,1,0:T(2,128)}), f32[8,2,4]{2,1,0:T(2,128)S(1)}, u32[]{:S(2)}, u32[]{:S(2)}) %all-to-all-start.1) | async-done | bytes 288 | tf_op jit(solution)/shard_map/all_to_all | solution.py:421
  192.5 0.7 fusion.1.slot
  193.2 0.6 reshape.111.shift
  193.8 15.7 %render.1 = f32[2,384,384]{2,1,0:T(8,128)} custom-call(s32[16]{0:T(128)} %fusion.1.slot, f32[32]{0:T(128)} %reshape.111.shift, f32[16,256,256]{2,1,0:T(8,128)} %all-to-all-done.blocks), custom_call_target="tpu_custom_call" | custom-call | tf_op jit(solution)/shard_map/render/pallas_call | solution.py:372
  209.5 0.0 copy-done.1
  209.5 0.7 copy.19
  (4 shorter events, 0.0 us)
Async XLA Ops:
  14.0 7.2 %copy-start.7 = (s32[4]{0:T(128)S(1)}, s32[4]{0:T(128)}, u32[]{:S(2)}) copy-start(s32[4]{0:T(128)} %constant.30.clone) | copy-start | bytes 52
  14.0 7.3 %copy-start.2 = (f32[4,4,32,256]{3,2,1,0:T(8,128)S(1)}, f32[4,4,32,256]{3,2,1,0:T(8,128)}, u32[]{:S(2)}) copy-start(f32[4,4,32,256]{3,2,1,0:T(8,128)} %param.13) | copy-start | bytes 1572868
  14.0 7.4 %copy-start = (f32[4,2,4,32,256]{4,3,2,1,0:T(8,128)S(1)}, f32[4,2,4,32,256]{4,3,2,1,0:T(8,128)}, u32[]{:S(2)}) copy-start(f32[4,2,4,32,256]{4,3,2,1,0:T(8,128)} %param.14) | copy-start | bytes 3145732
  14.0 7.5 %copy-start.3 = (f32[2,4,32,256]{3,2,1,0:T(8,128)S(1)}, f32[2,4,32,256]{3,2,1,0:T(8,128)}, u32[]{:S(2)}) copy-start(f32[2,4,32,256]{3,2,1,0:T(8,128)} %param.12) | copy-start | bytes 786436
  14.0 168.8 %all-to-all-start = ((f32[16,256,256]{2,1,0:T(8,128)}), f32[16,256,256]{2,1,0:T(8,128)}, u32[]{:S(2)}, u32[]{:S(2)}) async-start(f32[16,256,256]{2,1,0:T(8,128)} %place.1), calls=%async_computation | async-start | bytes 8388608 | tf_op jit(solution)/shard_map/all_to_all | solution.py:402
  20.4 2.2 %copy-start.5 = (s32[2,8]{1,0:T(2,128)S(1)}, s32[2,8]{1,0:T(2,128)}, u32[]{:S(2)}) copy-start(s32[2,8]{1,0:T(2,128)} %param.16) | copy-start | bytes 196
  21.4 161.1 %copy-start.6 = (s32[1,8]{1,0:T(1,128)S(1)}, s32[1,8]{1,0:T(1,128)}, u32[]{:S(2)}) copy-start(s32[1,8]{1,0:T(1,128)} %param.20) | copy-start | bytes 100
  21.4 161.2 %copy-start.4 = (s32[1,8,2]{1,2,0:T(2,128)S(1)}, s32[1,8,2]{1,2,0:T(2,128)}, u32[]{:S(2)}) copy-start(s32[1,8,2]{1,2,0:T(2,128)} %param.21) | copy-start | bytes 196
  180.0 29.6 %copy-start.1 = (f32[2,4,4,8,256]{4,3,2,1,0:T(8,128)S(1)}, f32[2,4,4,8,256]{4,3,2,1,0:T(8,128)}, u32[]{:S(2)}) copy-start(f32[2,4,4,8,256]{4,3,2,1,0:T(8,128)} %relax.1) | copy-start | bytes 786436
  183.4 9.0 %all-to-all-start.1 = ((f32[8,2,4]{2,1,0:T(2,128)}), f32[8,2,4]{2,1,0:T(2,128)S(1)}, u32[]{:S(2)}, u32[]{:S(2)}) async-start(f32[8,2,4]{2,1,0:T(2,128)} %bitcast.10), calls=%async_computation.1 | async-start | bytes 16384 | tf_op jit(solution)/shard_map/all_to_all | solution.py:421
